TPU v7x, 32 devices: a whole 2x2x4 slice. The times are simulated.
32 devices in a mesh: dp: 2 (over y), ctx: 4 (over x, core), tensor: 4 (over z).
Axes of the slice: x: 2, y: 2, z: 4, core: 2. Of those that a mesh axis runs over, the one named last changes fastest.
Arguments:
- residual: bfloat16 [2048, 3584], P(('dp', 'ctx', 'tensor')), parts along dimension 0, may hold values from -6 to 6
- queries: bfloat16 [2048, 1024], P(('dp', 'ctx'), 'tensor'), parts along dimension 0, may hold values from -8 to 8
- key_heads: bfloat16 [2048, 512], P(('dp', 'ctx'), 'tensor'), parts along dimension 0, may hold values from -8 to 8
- value_heads: bfloat16 [2048, 512], P(('dp', 'ctx'), 'tensor'), parts along dimension 0, may hold values from -6 to 6
- doc_blocks: int32 [12], P('dp'), parts along dimension 0, may hold values from 1 to 16, 32 in all
- out_weight: bfloat16 [1024, 3584], P('tensor'), may hold values from -0.53125 to 0.53125
- post_gain: float32 [3584], replicated, may hold values from 0.1 to 1.9
- ffn_gain: float32 [3584], replicated, may hold values from 0.1 to 1.9
- gate_weight: bfloat16 [3584, 3584], P('ctx', 'tensor'), may hold values from -0.09375 to 0.09375
- up_weight: bfloat16 [3584, 3584], P('ctx', 'tensor'), may hold values from -0.09375 to 0.09375
Outputs:
- mixed_stream: bfloat16 [2048, 3584], P(('dp', 'ctx', 'tensor')), parts along dimension 0
- ffn_hidden: bfloat16 [2048, 3584], P(('dp', 'ctx'), 'tensor'), parts along dimension 0
There are 2 independent parts, one for each index of `dp`. A program takes and returns all parts, laid end to end along the dimension named above; an argument that names none is the same for every part. Nothing has to cross between parts.
Inputs may be any that keep to these rules, and one draw needn't show every extreme that they name: `doc_blocks`: the lengths, in blocks of 32 positions, of the 6 documents packed in order into the sequence; they sum to 32, and the longest has exactly 16 blocks.
All inputs are finite; a program needn't handle non-finite values.
Results may differ from a plain program's by a relative error of at most 0.025.
Values may be sent and summed in bfloat16 or wider, within the bound.
A program may use at most 64 MiB of HBM per device.

v0:
```python
import jax
import jax.numpy as jnp
from jax import lax
from jax.sharding import PartitionSpec as P

BLOCK = 32
SOFT_CAP = 50.0
NORM_EPS = 1e-06
ROPE_BASE = 10000.0


def partner_2(value, axis, apart):
    mask = 2**apart
    pairs = [(source, source ^ mask) for source in range(lax.axis_size(axis))]
    return lax.ppermute(value, axis, pairs)


def rope_angles(positions, head_size):
    halfway = head_size // 2
    frequency = ROPE_BASE ** (-(jnp.arange(halfway, dtype=jnp.float32) * 2.0) / head_size)
    angles = positions.astype(jnp.float32)[:, None] * frequency[None, :]
    return (jnp.cos(angles), jnp.sin(angles))


def rotate(heads_in, cosine, sine_value, head_size):
    rows_here = heads_in.shape[0]
    reshaped = heads_in.astype(jnp.float32).reshape(rows_here, -1, head_size)
    leading = reshaped[:, :, : head_size // 2]
    trailing = reshaped[:, :, head_size // 2 :]
    cos_wide = cosine[:, None, :]
    sin_wide = sine_value[:, None, :]
    turned = jnp.concatenate(
        [leading * cos_wide - trailing * sin_wide, trailing * cos_wide + leading * sin_wide], axis=2
    )
    return turned.reshape(rows_here, -1).astype(jnp.bfloat16)


def doc_of(positions, doc_blocks):
    doc_ends = jnp.cumsum(doc_blocks)
    passed = positions[:, None] // BLOCK >= doc_ends[None, :]
    return jnp.sum(passed.astype(jnp.int32), axis=1)


def rms_scale(values):
    return values * lax.rsqrt(jnp.mean(values * values, axis=-1, keepdims=True) + NORM_EPS)


def gelu_gate(gate_sum, up_sum):
    return (jax.nn.gelu(gate_sum, approximate=True) * up_sum).astype(jnp.bfloat16)


def attend(query_rows, query_pos, query_doc, key_rows, value_rows, key_pos, key_doc, score_scale):
    scores = (
        lax.dot_general(
            query_rows, key_rows, (((1,), (1,)), ((), ())), preferred_element_type=jnp.float32
        )
        * score_scale
    )
    capped = SOFT_CAP * jnp.tanh(scores / SOFT_CAP)
    visible = (key_pos[None, :] <= query_pos[:, None]) & (key_doc[None, :] == query_doc[:, None])
    weights = jnp.where(visible, jnp.exp(capped), 0.0).astype(jnp.bfloat16)
    numerator = jnp.dot(weights, value_rows, preferred_element_type=jnp.float32)
    denominator = jnp.sum(weights.astype(jnp.float32), axis=1)
    return (numerator, denominator)


def join_halves(own_part, other_part, own_first):
    return jnp.where(
        own_first,
        jnp.concatenate([own_part, other_part], axis=2),
        jnp.concatenate([other_part, own_part], axis=2),
    )


def per_device(
    residual,
    queries,
    key_heads,
    value_heads,
    doc_blocks,
    out_weight,
    post_gain,
    ffn_gain,
    gate_weight,
    up_weight,
):
    tok_rows = queries.shape[0]
    head_size = queries.shape[1]
    score_scale = head_size ** (-0.5)
    query_pos = lax.axis_index("ctx") * tok_rows + jnp.arange(tok_rows, dtype=jnp.int32)
    query_doc = doc_of(query_pos, doc_blocks)
    cosine, sine_value = rope_angles(query_pos, head_size)
    query_rot = rotate(queries, cosine, sine_value, head_size)
    stacked = jnp.stack([key_heads, value_heads])
    own_first = lax.axis_index("tensor") % 2 == 0
    partner = partner_2(stacked, "tensor", 0)
    joined = join_halves(stacked, partner, own_first)
    key_rot = rotate(joined[0], cosine, sine_value, head_size)
    shard_pair = (
        lax.all_gather(key_rot, "ctx", axis=0, tiled=True),
        lax.all_gather(joined[1], "ctx", axis=0, tiled=True),
    )
    key_pos = jnp.arange(shard_pair[0].shape[0], dtype=jnp.int32)
    numerator, denominator = attend(
        query_rot,
        query_pos,
        query_doc,
        shard_pair[0],
        shard_pair[1],
        key_pos,
        doc_of(key_pos, doc_blocks),
        score_scale,
    )
    attended = (numerator / denominator[:, None]).astype(jnp.bfloat16)
    attn_rows = lax.psum_scatter(
        jnp.dot(attended, out_weight, preferred_element_type=jnp.float32).astype(jnp.bfloat16),
        "tensor",
        scatter_dimension=0,
        tiled=True,
    ).astype(jnp.float32)
    mixed_stream = (residual.astype(jnp.float32) + rms_scale(attn_rows) * post_gain).astype(
        jnp.bfloat16
    )
    ffn_input = (rms_scale(mixed_stream.astype(jnp.float32)) * ffn_gain).astype(jnp.bfloat16)
    gathered_rows = lax.all_gather(ffn_input, "tensor", axis=0, tiled=True)
    shard_pair = (
        lax.all_gather(gate_weight, "ctx", axis=0, tiled=True),
        lax.all_gather(up_weight, "ctx", axis=0, tiled=True),
    )
    gate_part = jnp.dot(gathered_rows, shard_pair[0], preferred_element_type=jnp.float32)
    up_part = jnp.dot(gathered_rows, shard_pair[1], preferred_element_type=jnp.float32)
    ffn_hidden = gelu_gate(gate_part, up_part)
    return (mixed_stream, ffn_hidden)


def solution(mesh):
    in_specs = (
        P(("dp", "ctx", "tensor"), None),
        P(("dp", "ctx"), "tensor"),
        P(("dp", "ctx"), "tensor"),
        P(("dp", "ctx"), "tensor"),
        P("dp"),
        P("tensor", None),
        P(),
        P(),
        P("ctx", "tensor"),
        P("ctx", "tensor"),
    )
    out_specs = (P(("dp", "ctx", "tensor"), None), P(("dp", "ctx"), "tensor"))
    return jax.shard_map(
        per_device, mesh=mesh, in_specs=in_specs, out_specs=out_specs, check_vma=False
    )
```

profile of v0, /device:TPU:0, one launch (start us, length us, event | category | flops | bytes accessed | tf_op | source)
XLA Modules:
  0.0 227.5 jit_solution(10332107046243191215)
XLA Ops:
  7.2 0.0 copy-start
  7.2 0.0 reduce-scatter.2.cloned.1.call-start
  7.2 1.0 pad_maximum_fusion
  8.2 3.1 %collective-permute-start = (bf16[2,256,128]{2,1,0:T(8,128)(2,1)S(1)}, bf16[2,256,128]{2,1,0:T(8,128)(2,1)S(1)}, u32[]{:S(2)}, u32[]{:S(2)}) collective-permute-start(bf16[2,256,128]{2,1,0:T(8,128)(2,1)S(1)} %pad_maximum_fusion), channel_id=1, source_target_pairs={{0,1},{1,0},{2,3},{3,2},{4,5},{5,4},{6,7},{7,6},{8,9},{9,8},{10,11... | collective-permute-start | bytes 393224 | tf_op jit(solution)/shard_map/ppermute | solution.py:15
  11.4 0.9 bitcast_convert_fusion
  12.3 0.8 reduce-window.8
  13.1 0.1 convert_reduce_fusion.2
  13.2 0.1 convert_reduce_fusion.1
  13.3 1.5 collective-permute-done
  14.9 1.0 maximum_select_fusion
  15.9 0.6 fusion.34
  16.5 7.3 %all-gather = bf16[1024,1,256]{2,0,1:T(8,128)(2,1)S(1)} all-gather(bf16[256,1,256]{2,0,1:T(8,128)(2,1)S(1)} %pad_maximum_fusion.1), channel_id=2, replica_groups=mesh['dp'=2,'ctx'=4,'tensor'=4] {'ctx'}, dimensions={0}, use_global_device_ids=true | all-gather | bytes 655360 | tf_op jit(solution)/shard_map/all_gather | solution.py:100
  23.9 7.3 %all-gather.1 = bf16[1,1024,256]{2,1,0:T(8,128)(2,1)S(1)} all-gather(bf16[1,256,256]{2,1,0:T(8,128)(2,1)S(1)} %get-tuple-element.8), channel_id=3, replica_groups=mesh['dp'=2,'ctx'=4,'tensor'=4] {'ctx'}, dimensions={1}, use_global_device_ids=true | all-gather | bytes 655360 | tf_op jit(solution)/shard_map/all_gather | solution.py:101
  31.1 0.7 convert_reduce_fusion
  31.8 0.0 copy-done
  31.8 2.4 %convolution_convert_fusion = bf16[256,3584]{1,0:T(8,128)(2,1)} fusion(bf16[256,3584]{1,0:T(8,128)(2,1)S(1)} %copy-done, bf16[256,1024]{1,0:T(8,128)(2,1)S(1)} %get-tuple-element.13, bf16[1,1024,256]{2,1,0:T(8,128)(2,1)S(1)} %all-gather.1, f32[256]{0:T(256)S(1)} %get-tuple-element.12), kind=kOutput, calls=%fused_computation | convolution fusion | flops 605028352 | bytes 4719616 | tf_op jit(solution)/shard_map/dot_general | solution.py:116
  34.2 0.0 copy-start.2
  34.2 0.0 copy-start.3
  34.2 0.0 copy-start.4
  34.2 0.0 reduce-scatter.2.cloned.1.call-update
  34.2 0.0 all-gather.6.cloned.1.call-start
  34.3 40.2 %reduce-scatter.2.cloned.1.call-done = bf16[64,3584]{1,0:T(8,128)(2,1)} async-done(((bf16[256,3584]{1,0:T(8,128)(2,1)}), bf16[64,3584]{1,0:T(8,128)(2,1)}) %reduce-scatter.2.cloned.1.call-update) | async-done | bytes 458768 | tf_op jit(solution)/shard_map/reduce_scatter | solution.py:115
  74.5 1.2 fusion.8
  75.7 0.0 copy-done.2
  75.7 0.0 copy-done.3
  75.7 1.4 fusion.12
  77.1 0.0 copy-start.1
  77.2 0.0 copy-done.4
  77.2 0.9 fusion.14
  78.1 0.0 all-gather.6.cloned.1.call-update
  78.1 0.0 all-gather.8.cloned.1.call-start
  78.2 0.7 all-gather.8.cloned.1.call-update
  78.9 0.0 all-gather.10.cloned.1.call-start
  78.9 0.5 all-gather.10.cloned.1.call-update
  79.5 0.0 copy-done.1
  79.5 39.2 %all-gather.6.cloned.1.call-done = bf16[256,3584]{1,0:T(8,128)(2,1)} async-done(((bf16[64,3584]{1,0:T(8,128)(2,1)}), bf16[256,3584]{1,0:T(8,128)(2,1)}) %all-gather.6.cloned.1.call-update) | async-done | bytes 1835024 | tf_op jit(solution)/shard_map/all_gather | solution.py:125
  118.7 47.5 %all-gather.8.cloned.1.call-done = bf16[3584,896]{1,0:T(8,128)(2,1)} async-done(((bf16[896,896]{1,0:T(8,128)(2,1)}), bf16[3584,896]{1,0:T(8,128)(2,1)}) %all-gather.8.cloned.1.call-update) | async-done | bytes 6422544 | tf_op jit(solution)/shard_map/all_gather | solution.py:127
  166.2 5.5 %fusion.52 = f32[256,896]{1,0:T(8,128)S(1)} fusion(bf16[256,3584]{1,0:T(8,128)(2,1)} %all-gather.6.cloned.1.call-done, bf16[3584,896]{1,0:T(8,128)(2,1)} %all-gather.8.cloned.1.call-done), kind=kOutput, calls=%fused_computation.83 | convolution fusion | flops 1644167168 | bytes 9175040 | tf_op jit(solution)/shard_map/dot_general | solution.py:130
  171.6 43.1 %all-gather.10.cloned.1.call-done = bf16[3584,896]{1,0:T(8,128)(2,1)} async-done(((bf16[896,896]{1,0:T(8,128)(2,1)}), bf16[3584,896]{1,0:T(8,128)(2,1)}) %all-gather.10.cloned.1.call-update) | async-done | bytes 6422544 | tf_op jit(solution)/shard_map/all_gather | solution.py:128
  214.7 6.3 %fusion.5 = bf16[256,896]{1,0:T(8,128)(2,1)} fusion(bf16[256,3584]{1,0:T(8,128)(2,1)} %all-gather.6.cloned.1.call-done, bf16[3584,896]{1,0:T(8,128)(2,1)} %all-gather.10.cloned.1.call-done, f32[256,896]{1,0:T(8,128)S(1)} %fusion.52), kind=kOutput, calls=%fused_computation.9 | convolution fusion | flops 1646460928 | bytes 9633792 | tf_op jit(solution)/shard_map/dot_general | solution.py:131
  (8 shorter events, 0.1 us)
Async XLA Ops:
  7.2 24.7 %copy-start = (bf16[256,3584]{1,0:T(8,128)(2,1)S(1)}, bf16[256,3584]{1,0:T(8,128)(2,1)}, u32[]{:S(2)}) copy-start(bf16[256,3584]{1,0:T(8,128)(2,1)} %param.15) | copy-start | bytes 5505028
  7.2 67.3 %reduce-scatter.2.cloned.1.call-start = ((), (), s32[]{:S(2)}) async-start(), calls=%async_computation.1 | async-start | bytes 2293760 | tf_op jit(solution)/shard_map/reduce_scatter | solution.py:115
  8.2 6.6 %collective-permute-start = (bf16[2,256,128]{2,1,0:T(8,128)(2,1)S(1)}, bf16[2,256,128]{2,1,0:T(8,128)(2,1)S(1)}, u32[]{:S(2)}, u32[]{:S(2)}) collective-permute-start(bf16[2,256,128]{2,1,0:T(8,128)(2,1)S(1)} %pad_maximum_fusion), channel_id=1, source_target_pairs={{0,1},{1,0},{2,3},{3,2},{4,5},{5,4},{6,7},{7,6},{8,9},{9,8},{10,11... | collective-permute-start | bytes 393224 | tf_op jit(solution)/shard_map/ppermute | solution.py:15
  34.2 41.5 %copy-start.2 = (bf16[64,3584]{1,0:T(8,128)(2,1)S(1)}, bf16[64,3584]{1,0:T(8,128)(2,1)}, u32[]{:S(2)}) copy-start(bf16[64,3584]{1,0:T(8,128)(2,1)} %param.10) | copy-start | bytes 1376260
  34.2 41.5 %copy-start.3 = (f32[3584]{0:T(1024)S(1)}, f32[3584]{0:T(1024)}, u32[]{:S(2)}) copy-start(f32[3584]{0:T(1024)} %param.16) | copy-start | bytes 43012
  34.2 43.0 %copy-start.4 = (f32[3584]{0:T(1024)S(1)}, f32[3584]{0:T(1024)}, u32[]{:S(2)}) copy-start(f32[3584]{0:T(1024)} %param.17) | copy-start | bytes 43012
  34.2 84.4 %all-gather.6.cloned.1.call-start = ((), (), s32[]{:S(2)}) async-start(), calls=%async_computation.2 | async-start | bytes 2293760 | tf_op jit(solution)/shard_map/all_gather | solution.py:125
  77.1 2.3 %copy-start.1 = (bf16[64,3584]{1,0:T(8,128)(2,1)}, bf16[64,3584]{1,0:T(8,128)(2,1)S(1)}, u32[]{:S(2)}) copy-start(bf16[64,3584]{1,0:T(8,128)(2,1)S(1)} %get-tuple-element.3) | copy-start | bytes 1376260
  78.1 88.0 %all-gather.8.cloned.1.call-start = ((), (), s32[]{:S(2)}) async-start(), calls=%async_computation.3 | async-start | bytes 8028160 | tf_op jit(solution)/shard_map/all_gather | solution.py:127
  78.9 135.9 %all-gather.10.cloned.1.call-start = ((), (), s32[]{:S(2)}) async-start(), calls=%async_computation.4 | async-start | bytes 8028160 | tf_op jit(solution)/shard_map/all_gather | solution.py:128
Sparse Core Ops, SparseCore 0:
  34.4 40.0 reduce-scatter.1
  78.3 40.3 all-gather.5
  120.2 45.9 all-gather.7
  167.6 47.0 all-gather.9
where the time goes:
time: 228 us
  waiting for transfers between devices  173 us (76%)
  matrix products  14.8 us (6%)
  blocking collectives  14.6 us (6%)
  between operations  13.9 us (6%)
  other arithmetic  8.2 us (4%)
  starting transfers between devices  3.28 us (1%)
    all_gather x1, waiting for transfers between devices, per_device(): lax.all_gather(gate_weight, 'ctx', axis=0, tiled=True)  47.5 us
    all_gather x1, waiting for transfers between devices, per_device(): lax.all_gather(up_weight, 'ctx', axis=0, tiled=True)  43.1 us
    reduce_scatter x1, waiting for transfers between devices, per_device(): lax.psum_scatter(jnp.dot(attended, out_weight, preferred_element_type=jnp...  40.2 us
    all_gather x1, waiting for transfers between devices, per_device(): gathered_rows = lax.all_gather(ffn_input, 'tensor', axis=0, tiled=True)  39.2 us
    all_gather x1, blocking collectives, per_device(): lax.all_gather(key_rot, 'ctx', axis=0, tiled=True)  7.34 us
    all_gather x1, blocking collectives, per_device(): lax.all_gather(joined[1], 'ctx', axis=0, tiled=True)  7.26 us
    dot_general x1, matrix products, per_device(): jnp.dot(gathered_rows, shard_pair[1], preferred_element_type=jnp.float32)  6.25 us
    dot_general x1, matrix products, per_device(): jnp.dot(gathered_rows, shard_pair[0], preferred_element_type=jnp.float32)  5.45 us
  transfers between devices with their start and end apart: 5, of which 5 were waited for; matrix products, arithmetic and copies ran while one was open for 3% of the time, Pallas kernels for 0%

commit v1 on v0

--- a/solution.py
+++ b/solution.py
@@ -122,7 +122,9 @@
         jnp.bfloat16
     )
     ffn_input = (rms_scale(mixed_stream.astype(jnp.float32)) * ffn_gain).astype(jnp.bfloat16)
-    gathered_rows = lax.all_gather(ffn_input, "tensor", axis=0, tiled=True)
+    gathered_rows = jnp.concatenate(
+        lax.all_to_all(jnp.stack([ffn_input] * lax.axis_size("tensor")), "tensor", 0, 0), axis=0
+    )
     shard_pair = (
         lax.all_gather(gate_weight, "ctx", axis=0, tiled=True),
         lax.all_gather(up_weight, "ctx", axis=0, tiled=True),

time: 228 us -> 147 us (0.64)
  waiting for transfers between devices: 173 us -> 45.3 us
  blocking collectives: 14.6 us -> 60.3 us
    all_gather x1, waiting for transfers between devices: 47.5 us -> 0.01 us  [per_device(): lax.all_gather(gate_weight, 'ctx', axis=0, tiled=True)]
    all_to_all x0 -> x1, blocking collectives: none -> 45.7 us  [per_device(): lax.all_to_all(jnp.stack([ffn_input] * lax.axis_size('tensor')), 'tensor'...]
    all_gather x1, waiting for transfers between devices: 43.1 us -> 3.64 us  [per_device(): lax.all_gather(up_weight, 'ctx', axis=0, tiled=True)]
    all_gather x1 -> x0, waiting for transfers between devices: 39.2 us -> none  [per_device(): gathered_rows = lax.all_gather(ffn_input, 'tensor', axis=0, tiled=True)]
  transfers between devices with their start and end apart: 5 -> 4, of which waited for: 5 -> 3; matrix products, arithmetic and copies ran while one was open for 3% -> 7% of each run, Pallas kernels for 0% -> 0%
where the time goes in v1:
time: 147 us
  blocking collectives  60.3 us (41%)
  waiting for transfers between devices  45.3 us (31%)
  between operations  15.6 us (11%)
  matrix products  14.8 us (10%)
  other arithmetic  7.47 us (5%)
  starting transfers between devices  3.24 us (2%)
    all_to_all x1, blocking collectives, per_device(): lax.all_to_all(jnp.stack([ffn_input] * lax.axis_size('tensor')), 'tensor'...  45.7 us
    reduce_scatter x1, waiting for transfers between devices, per_device(): lax.psum_scatter(jnp.dot(attended, out_weight, preferred_element_type=jnp...  39 us
    all_gather x1, blocking collectives, per_device(): lax.all_gather(key_rot, 'ctx', axis=0, tiled=True)  7.34 us
    all_gather x1, blocking collectives, per_device(): lax.all_gather(joined[1], 'ctx', axis=0, tiled=True)  7.26 us
    dot_general x1, matrix products, per_device(): jnp.dot(gathered_rows, shard_pair[1], preferred_element_type=jnp.float32)  6.25 us
    dot_general x1, matrix products, per_device(): jnp.dot(gathered_rows, shard_pair[0], preferred_element_type=jnp.float32)  5.45 us
    all_gather x1, waiting for transfers between devices, per_device(): lax.all_gather(up_weight, 'ctx', axis=0, tiled=True)  3.64 us
    ppermute x1, starting transfers between devices, partner_2(): return lax.ppermute(value, axis, pairs)  3.12 us
  transfers between devices with their start and end apart: 4, of which 3 were waited for; matrix products, arithmetic and copies ran while one was open for 7% of the time, Pallas kernels for 0%

profile of v1, /device:TPU:0, one launch (start us, length us, event | category | flops | bytes accessed | tf_op | source)
XLA Modules:
  0.0 146.8 jit_solution(14910882615770059241)
XLA Ops:
  8.0 0.0 copy-start
  8.0 0.0 reduce-scatter.2.cloned.1.call-start
  8.1 1.0 pad_maximum_fusion
  9.1 3.1 %collective-permute-start = (bf16[2,256,128]{2,1,0:T(8,128)(2,1)S(1)}, bf16[2,256,128]{2,1,0:T(8,128)(2,1)S(1)}, u32[]{:S(2)}, u32[]{:S(2)}) collective-permute-start(bf16[2,256,128]{2,1,0:T(8,128)(2,1)S(1)} %pad_maximum_fusion), channel_id=1, source_target_pairs={{0,1},{1,0},{2,3},{3,2},{4,5},{5,4},{6,7},{7,6},{8,9},{9,8},{10,11... | collective-permute-start | bytes 393224 | tf_op jit(solution)/shard_map/ppermute | solution.py:15
  12.2 0.9 bitcast_convert_fusion
  13.1 0.8 reduce-window.8
  14.0 0.1 convert_reduce_fusion.2
  14.1 0.1 convert_reduce_fusion.1
  14.2 1.5 %collective-permute-done = bf16[2,256,128]{2,1,0:T(8,128)(2,1)S(1)} collective-permute-done((bf16[2,256,128]{2,1,0:T(8,128)(2,1)S(1)}, bf16[2,256,128]{2,1,0:T(8,128)(2,1)S(1)}, u32[]{:S(2)}, u32[]{:S(2)}) %collective-permute-start) | collective-permute-done | bytes 131104 | tf_op jit(solution)/shard_map/ppermute | solution.py:15
  15.7 1.0 maximum_select_fusion
  16.7 0.6 fusion.34
  17.4 7.3 %all-gather = bf16[1024,1,256]{2,0,1:T(8,128)(2,1)S(1)} all-gather(bf16[256,1,256]{2,0,1:T(8,128)(2,1)S(1)} %pad_maximum_fusion.1), channel_id=2, replica_groups=mesh['dp'=2,'ctx'=4,'tensor'=4] {'ctx'}, dimensions={0}, use_global_device_ids=true | all-gather | bytes 655360 | tf_op jit(solution)/shard_map/all_gather | solution.py:100
  24.7 7.3 %all-gather.1 = bf16[1,1024,256]{2,1,0:T(8,128)(2,1)S(1)} all-gather(bf16[1,256,256]{2,1,0:T(8,128)(2,1)S(1)} %get-tuple-element.8), channel_id=3, replica_groups=mesh['dp'=2,'ctx'=4,'tensor'=4] {'ctx'}, dimensions={1}, use_global_device_ids=true | all-gather | bytes 655360 | tf_op jit(solution)/shard_map/all_gather | solution.py:101
  32.0 0.7 convert_reduce_fusion
  32.7 0.0 copy-done
  32.7 2.4 %convolution_convert_fusion = bf16[256,3584]{1,0:T(8,128)(2,1)} fusion(bf16[256,3584]{1,0:T(8,128)(2,1)S(1)} %copy-done, bf16[256,1024]{1,0:T(8,128)(2,1)S(1)} %get-tuple-element.13, bf16[1,1024,256]{2,1,0:T(8,128)(2,1)S(1)} %all-gather.1, f32[256]{0:T(256)S(1)} %get-tuple-element.12), kind=kOutput, calls=%fused_computation | convolution fusion | flops 605028352 | bytes 4719616 | tf_op jit(solution)/shard_map/dot_general | solution.py:116
  35.1 0.0 reduce-scatter.2.cloned.1.call-update
  35.1 0.0 copy-start.2
  35.1 0.0 copy-start.3
  35.1 0.0 all-gather.5.cloned.1.call-start
  35.2 0.5 all-gather.5.cloned.1.call-update
  35.7 0.0 copy-start.4
  35.7 0.0 all-gather.7.cloned.1.call-start
  35.7 0.5 all-gather.7.cloned.1.call-update
  36.3 39.0 %reduce-scatter.2.cloned.1.call-done = bf16[64,3584]{1,0:T(8,128)(2,1)} async-done(((bf16[256,3584]{1,0:T(8,128)(2,1)}), bf16[64,3584]{1,0:T(8,128)(2,1)}) %reduce-scatter.2.cloned.1.call-update) | async-done | bytes 458768 | tf_op jit(solution)/shard_map/reduce_scatter | solution.py:115
  75.3 1.2 fusion.8
  76.6 0.0 copy-done.2
  76.6 0.0 copy-done.3
  76.6 1.4 fusion.12
  78.0 0.0 copy-start.1
  78.0 0.0 copy-done.4
  78.1 0.2 fusion.14
  78.2 0.1 stack.19
  78.4 45.7 %all_to_all.5 = bf16[4,64,3584]{2,1,0:T(8,128)(2,1)} all-to-all(bf16[4,64,3584]{2,1,0:T(8,128)(2,1)S(1)} %stack.19), channel_id=1, replica_groups=mesh['dp'=2,'ctx'=4,'tensor'=4] {'tensor'}, dimensions={0} | all-to-all | bytes 3670016 | tf_op jit(solution)/shard_map/all_to_all | solution.py:126
  124.0 0.0 copy-done.1
  124.0 0.0 all-gather.5.cloned.1.call-done
  124.0 5.4 %fusion.52 = f32[256,896]{1,0:T(8,128)S(1)} fusion(bf16[256,3584]{1,0:T(8,128)(2,1)} %bitcast.33, bf16[3584,896]{1,0:T(8,128)(2,1)} %all-gather.5.cloned.1.call-done), kind=kOutput, calls=%fused_computation.83 | convolution fusion | flops 1644167168 | bytes 9175040 | tf_op jit(solution)/shard_map/dot_general | solution.py:132
  129.5 3.6 %all-gather.7.cloned.1.call-done = bf16[3584,896]{1,0:T(8,128)(2,1)} async-done(((bf16[896,896]{1,0:T(8,128)(2,1)}), bf16[3584,896]{1,0:T(8,128)(2,1)}) %all-gather.7.cloned.1.call-update) | async-done | bytes 6422544 | tf_op jit(solution)/shard_map/all_gather | solution.py:130
  133.1 6.3 %fusion.5 = bf16[256,896]{1,0:T(8,128)(2,1)} fusion(bf16[256,3584]{1,0:T(8,128)(2,1)} %bitcast.34, bf16[3584,896]{1,0:T(8,128)(2,1)} %all-gather.7.cloned.1.call-done, f32[256,896]{1,0:T(8,128)S(1)} %fusion.52), kind=kOutput, calls=%fused_computation.9 | convolution fusion | flops 1646460928 | bytes 9633792 | tf_op jit(solution)/shard_map/dot_general | solution.py:133
  (8 shorter events, 0.1 us)
Async XLA Ops:
  8.0 24.7 %copy-start = (bf16[256,3584]{1,0:T(8,128)(2,1)S(1)}, bf16[256,3584]{1,0:T(8,128)(2,1)}, u32[]{:S(2)}) copy-start(bf16[256,3584]{1,0:T(8,128)(2,1)} %param.15) | copy-start | bytes 5505028
  8.0 67.3 %reduce-scatter.2.cloned.1.call-start = ((), (), s32[]{:S(2)}) async-start(), calls=%async_computation.2 | async-start | bytes 2293760 | tf_op jit(solution)/shard_map/reduce_scatter | solution.py:115
  9.1 6.6 %collective-permute-start = (bf16[2,256,128]{2,1,0:T(8,128)(2,1)S(1)}, bf16[2,256,128]{2,1,0:T(8,128)(2,1)S(1)}, u32[]{:S(2)}, u32[]{:S(2)}) collective-permute-start(bf16[2,256,128]{2,1,0:T(8,128)(2,1)S(1)} %pad_maximum_fusion), channel_id=1, source_target_pairs={{0,1},{1,0},{2,3},{3,2},{4,5},{5,4},{6,7},{7,6},{8,9},{9,8},{10,11... | collective-permute-start | bytes 393224 | tf_op jit(solution)/shard_map/ppermute | solution.py:15
  35.1 41.5 %copy-start.2 = (bf16[64,3584]{1,0:T(8,128)(2,1)S(1)}, bf16[64,3584]{1,0:T(8,128)(2,1)}, u32[]{:S(2)}) copy-start(bf16[64,3584]{1,0:T(8,128)(2,1)} %param.10) | copy-start | bytes 1376260
  35.1 41.5 %copy-start.3 = (f32[3584]{0:T(1024)S(1)}, f32[3584]{0:T(1024)}, u32[]{:S(2)}) copy-start(f32[3584]{0:T(1024)} %param.16) | copy-start | bytes 43012
  35.1 88.9 %all-gather.5.cloned.1.call-start = ((), (), s32[]{:S(2)}) async-start(), calls=%async_computation.3 | async-start | bytes 8028160 | tf_op jit(solution)/shard_map/all_gather | solution.py:129
  35.7 42.4 %copy-start.4 = (f32[3584]{0:T(1024)S(1)}, f32[3584]{0:T(1024)}, u32[]{:S(2)}) copy-start(f32[3584]{0:T(1024)} %param.17) | copy-start | bytes 43012
  35.7 97.4 %all-gather.7.cloned.1.call-start = ((), (), s32[]{:S(2)}) async-start(), calls=%async_computation.4 | async-start | bytes 8028160 | tf_op jit(solution)/shard_map/all_gather | solution.py:130
  78.0 46.0 %copy-start.1 = (bf16[64,3584]{1,0:T(8,128)(2,1)}, bf16[64,3584]{1,0:T(8,128)(2,1)S(1)}, u32[]{:S(2)}) copy-start(bf16[64,3584]{1,0:T(8,128)(2,1)S(1)} %get-tuple-element.3) | copy-start | bytes 1376260
Sparse Core Ops, SparseCore 0:
  35.2 40.0 reduce-scatter.1
Sparse Core Ops, SparseCore 1:
  37.1 47.5 all-gather.4
  86.1 46.9 all-gather.6
